TPU v7x, 512 devices: a whole 4x8x8 slice. The times are simulated.
512 devices in a mesh: shard: 128 (over y, z_hi, x), tensor: 4 (over z_lo, core).
Axes of the slice: x: 4, y: 8, z: 8 (z_hi: 4, z_lo: 2; z = z_hi * 2 + z_lo), core: 2. Of those that a mesh axis runs over, the one named last changes fastest.
Arguments:
- gradients: bfloat16 [128, 128, 32, 512], P('shard', None, 'tensor'), may hold values from -2 to 2
- master_weights: float32 [128, 32, 512], P('shard', 'tensor'), may hold values from -6 to 6
- first_moment: float32 [128, 32, 512], P('shard', 'tensor'), may hold values from -4 to 4
- second_moment: float32 [128, 32, 512], P('shard', 'tensor'), may hold values from 0.5 to 4
- old_basis: float32 [128, 512, 512], P('shard', 'tensor')
- old_stats: float32 [128, 512, 512], P('shard', 'tensor'), as said below
- owner_table: int32 [128], replicated, may hold values from 0 to 127, each once
Outputs:
- updated_weights: float32 [128, 32, 512], P(None, 'tensor')
- new_first: float32 [128, 32, 512], P('shard', 'tensor')
- new_second: float32 [128, 32, 512], P('shard', 'tensor')
- new_basis: float32 [128, 512, 512], P('shard', 'tensor')
- new_stats: float32 [128, 512, 512], P('shard', 'tensor')
Inputs may be any that keep to these rules, and one draw needn't show every extreme that they name: owner_table names every owner 0 to 127 exactly once. `old_stats`: each block's matrix is symmetric.
All inputs are finite; a program needn't handle non-finite values.
Results may differ from a plain program's by a relative error of at most 0.004.
Values may be sent and summed in bfloat16 or wider, within the bound.
No kernel may reach another device: no remote copies, remote signals or barrier semaphores. Data moves between devices by JAX's collectives and lax.ppermute only.
A program may use at most 64 MiB of HBM per device.

v0:
```python
import jax
import jax.numpy as jnp
from jax import lax
from jax.sharding import PartitionSpec as P

NS_ITERS = 3


momentum_decay = 0.9
square_decay = 0.95
stats_decay = 0.95
step_size = 0.05
start_gain = 1.7
epsilon = 1e-06


def gram_of(matrix):
    return lax.dot_general(
        matrix, matrix, (((0,), (0,)), ((), ())), precision=lax.Precision.HIGHEST
    )


def body(gradients, master_weights, first_moment, second_moment, old_basis, old_stats, owner_table):
    highest = lax.Precision.HIGHEST
    blocks = owner_table.shape[0]
    places = jnp.arange(blocks, dtype=jnp.int32)
    inverse = jnp.sum(
        jnp.where(owner_table[None, :] == places[:, None], places[None, :], 0), axis=1
    )
    ordered = jnp.take(gradients[0], inverse, axis=0)
    summed = lax.psum_scatter(
        ordered.astype(jnp.float32), "shard", scatter_dimension=0, tiled=True
    )[0]
    whole_basis = lax.all_gather(old_basis[0], "tensor", axis=0, tiled=True)
    turned = jnp.dot(summed, whole_basis, precision=highest)
    first_new = momentum_decay * first_moment[0] + (1.0 - momentum_decay) * turned
    second_new = square_decay * second_moment[0] + (1.0 - square_decay) * turned * turned
    direction = first_new / jnp.sqrt(second_new)
    rotated_back = lax.dot_general(
        direction, whole_basis, (((1,), (1,)), ((), ())), precision=highest
    )
    weight_new = master_weights[0] - step_size * rotated_back
    gathered = lax.all_gather(weight_new[None], "shard", axis=0, tiled=True)
    updated_weights = jnp.take(gathered, owner_table, axis=0)
    rows_here = old_basis.shape[1]
    position = lax.axis_index("tensor") * rows_here
    whole_grad = lax.all_gather(summed, "tensor", axis=0, tiled=True)
    own_columns = lax.dynamic_slice_in_dim(whole_grad, position, rows_here, 1)
    fresh_term = lax.dot_general(
        own_columns, whole_grad, (((0,), (0,)), ((), ())), precision=highest
    )
    stats_new = stats_decay * old_stats[0] + (1.0 - stats_decay) * fresh_term
    power_part = jnp.dot(stats_new, whole_basis, precision=highest)
    whole_power = lax.all_gather(power_part, "tensor", axis=0, tiled=True)
    gram_matrix = gram_of(whole_power)
    factor = start_gain / jnp.sqrt(jnp.trace(gram_matrix) + epsilon)
    current = whole_power * factor
    gram_matrix = gram_matrix * (factor * factor)
    for sweep in range(NS_ITERS):
        if sweep > 0:
            gram_matrix = gram_of(current)
        if sweep + 1 < NS_ITERS:
            current = 1.5 * current - 0.5 * jnp.dot(current, gram_matrix, precision=highest)
        else:
            own_rows = lax.dynamic_slice_in_dim(current, position, rows_here, 0)
            current = 1.5 * own_rows - 0.5 * jnp.dot(own_rows, gram_matrix, precision=highest)
    return (updated_weights, first_new[None], second_new[None], current[None], stats_new[None])


def solution(mesh):
    return jax.shard_map(
        body,
        mesh=mesh,
        in_specs=(
            P("shard", None, "tensor", None),
            P("shard", "tensor", None),
            P("shard", "tensor", None),
            P("shard", "tensor", None),
            P("shard", "tensor", None),
            P("shard", "tensor", None),
            P(),
        ),
        out_specs=(
            P(None, "tensor", None),
            P("shard", "tensor", None),
            P("shard", "tensor", None),
            P("shard", "tensor", None),
            P("shard", "tensor", None),
        ),
        check_vma=False,
    )
```

profile of v0, /device:TPU:1, one launch (start us, length us, event | category | flops | bytes accessed | tf_op | source)
XLA Modules:
  0.0 950.2 jit_solution(6312819126764942959)
XLA Ops:
  8.0 0.0 copy-start
  8.0 0.0 reduce-scatter.2.cloned.1.call-start
  8.1 0.8 select_reduce_fusion.1
  8.9 0.3 copy-done
  9.2 0.6 gather_fusion
  9.9 0.0 copy-start.4
  9.9 1.5 select_convert_fusion
  11.5 0.0 reduce-scatter.2.cloned.1.call-update
  11.5 0.0 copy-start.5
  11.5 0.0 copy-start.6
  11.5 0.0 copy-start.8
  11.5 0.0 all-gather.9.cloned.1.call-start
  11.6 0.5 all-gather.9.cloned.1.call-update
  12.1 0.0 all-gather.7.cloned.1.call-start
  12.1 667.6 %reduce-scatter.2.cloned.1.call-done = f32[1,8,512]{2,1,0:T(8,128)} async-done(((f32[128,8,512]{2,1,0:T(8,128)}), f32[1,8,512]{2,1,0:T(8,128)}) %reduce-scatter.2.cloned.1.call-update) | async-done | bytes 16400 | tf_op jit(solution)/shard_map/reduce_scatter | solution.py:31
  679.8 0.0 copy-start.7
  679.8 111.8 %all-gather.2 = f32[1,32,512]{2,1,0:T(8,128)S(1)} all-gather(f32[1,8,512]{2,1,0:T(8,128)} %reduce-scatter.2.cloned.1.call-done), channel_id=4, replica_groups=mesh['shard'=128,'tensor'=4] {'tensor'}, dimensions={1}, use_global_device_ids=true | all-gather | bytes 81920 | tf_op jit(solution)/shard_map/all_gather | solution.py:47
  791.6 0.0 copy-done.4
  791.6 0.4 fusion.2
  792.0 0.0 copy-start.3
  792.1 0.0 copy-start.9
  792.1 0.0 all-gather.9.cloned.1.call-done
  792.1 0.0 copy-start.1
  792.1 2.7 fusion.6
  794.8 0.0 all-gather.7.cloned.1.call-update
  794.9 0.0 all-gather.11.cloned.1.call-start
  794.9 0.0 copy-done.7
  794.9 0.0 copy-done.1
  794.9 0.6 fusion.9
  795.5 0.0 copy-done.5
  795.5 0.0 copy-done.6
  795.6 0.0 copy-done.8
  795.6 1.6 fusion.5
  797.1 0.0 all-gather.11.cloned.1.call-update
  797.2 0.0 copy-done.9
  797.2 0.6 fusion.24
  797.8 14.4 %all-gather.7.cloned.1.call-done = f32[512,512]{1,0:T(8,128)} async-done(((f32[128,512]{1,0:T(8,128)}), f32[512,512]{1,0:T(8,128)}) %all-gather.7.cloned.1.call-update) | async-done | bytes 1048592 | tf_op jit(solution)/shard_map/all_gather | solution.py:54
  812.3 0.0 copy-start.2
  812.3 4.1 select_reduce_fusion
  816.3 0.0 copy-done.3
  817.0 0.0 copy-done.2
  817.0 1.9 fusion.1
  819.0 1.9 fusion.33
  820.9 1.9 fusion
  822.7 1.9 fusion.34
  824.6 1.4 fusion.4
  826.0 112.8 %all-gather.11.cloned.1.call-done = f32[1024,512]{1,0:T(8,128)} async-done(((f32[8,512]{1,0:T(8,128)}), f32[1024,512]{1,0:T(8,128)}) %all-gather.11.cloned.1.call-update) | async-done | bytes 2097168 | tf_op jit(solution)/shard_map/all_gather | solution.py:43
  938.8 2.3 gather_fusion.1
  941.1 1.5 broadcast_select_fusion
  (6 shorter events, 0.0 us)
Async XLA Ops:
  8.0 1.2 copy-start
  8.0 671.8 %reduce-scatter.2.cloned.1.call-start = ((), (), s32[]{:S(2)}) async-start(), calls=%async_computation.1 | async-start | bytes 2113536 | tf_op jit(solution)/shard_map/reduce_scatter | solution.py:31
  9.9 781.7 %copy-start.4 = (f32[1,128,512]{2,1,0:T(8,128)S(1)}, f32[1,128,512]{2,1,0:T(8,128)}, u32[]{:S(2)}) copy-start(f32[1,128,512]{2,1,0:T(8,128)} %param.12) | copy-start | bytes 786436
  11.5 784.1 %copy-start.5 = (f32[1,8,512]{2,1,0:T(8,128)S(1)}, f32[1,8,512]{2,1,0:T(8,128)}, u32[]{:S(2)}) copy-start(f32[1,8,512]{2,1,0:T(8,128)} %param.9) | copy-start | bytes 49156
  11.5 784.1 %copy-start.6 = (f32[1,8,512]{2,1,0:T(8,128)S(1)}, f32[1,8,512]{2,1,0:T(8,128)}, u32[]{:S(2)}) copy-start(f32[1,8,512]{2,1,0:T(8,128)} %param.10) | copy-start | bytes 49156
  11.5 784.1 %copy-start.8 = (f32[1,8,512]{2,1,0:T(8,128)S(1)}, f32[1,8,512]{2,1,0:T(8,128)}, u32[]{:S(2)}) copy-start(f32[1,8,512]{2,1,0:T(8,128)} %param.8) | copy-start | bytes 49156
  11.5 780.6 %all-gather.9.cloned.1.call-start = ((), (), s32[]{:S(2)}) async-start(), calls=%async_computation.3 | async-start | bytes 1310720 | tf_op jit(solution)/shard_map/all_gather | solution.py:34
  12.1 800.2 %all-gather.7.cloned.1.call-start = ((), (), s32[]{:S(2)}) async-start(), calls=%async_computation.2 | async-start | bytes 1310720 | tf_op jit(solution)/shard_map/all_gather | solution.py:54
  679.8 115.1 %copy-start.7 = (f32[1,8,512]{2,1,0:T(8,128)S(1)}, f32[1,8,512]{2,1,0:T(8,128)}, u32[]{:S(2)}) copy-start(f32[1,8,512]{2,1,0:T(8,128)} %reduce-scatter.2.cloned.1.call-done) | copy-start | bytes 49156
  792.0 24.3 %copy-start.3 = (f32[128,512]{1,0:T(8,128)}, f32[128,512]{1,0:T(8,128)S(1)}, u32[]{:S(2)}) copy-start(f32[128,512]{1,0:T(8,128)S(1)} %fusion.2) | copy-start | bytes 786436
  792.1 5.1 copy-start.9
  792.1 2.8 copy-start.1
  794.9 143.9 %all-gather.11.cloned.1.call-start = ((), (), s32[]{:S(2)}) async-start(), calls=%async_computation.4 | async-start | bytes 2113536 | tf_op jit(solution)/shard_map/all_gather | solution.py:43
  812.3 4.8 copy-start.2
Sparse Core Ops, SparseCore 0:
  12.2 667.5 reduce-scatter.1
Sparse Core Ops, SparseCore 1:
  14.1 32.4 all-gather.8
  795.0 17.3 all-gather.6
  817.2 121.5 all-gather.10
where the time goes:
time: 953 us; the launch traced here: 950 us
  waiting for transfers between devices  795 us (83%)
  blocking collectives  112 us (12%)
  matrix products  18.4 us (2%)
  between operations  16.6 us (2%)
    reduce_scatter x1, waiting for transfers between devices, body(): lax.psum_scatter(ordered.astype(jnp.float32), 'shard', scatter_dimension=...  668 us
    all_gather x1, waiting for transfers between devices, body(): gathered = lax.all_gather(weight_new[None], 'shard', axis=0, tiled=True)  113 us
    all_gather x1, blocking collectives, body(): whole_grad = lax.all_gather(summed, 'tensor', axis=0, tiled=True)  112 us
  transfers between devices with their start and end apart: 4, of which 3 were waited for; matrix products, arithmetic and copies ran while one was open for 2% of the time, Pallas kernels for 0%

commit v1 on v0

v1 whole, which is shorter than its diff:
```python
import jax
import jax.numpy as jnp
from jax import lax
from jax.sharding import PartitionSpec as P

NS_ITERS = 3

momentum_decay = 0.9
square_decay = 0.95
stats_decay = 0.95
step_size = 0.05
start_gain = 1.7
epsilon = 1e-06

NY, NZ, NX = 8, 4, 4
NYZ = NY * NZ
NT = 4
X_GROUPS = [[yz * NX + x for x in range(NX)] for yz in range(NYZ)]
YZ_GROUPS = [[yz * NX + x for yz in range(NYZ)] for x in range(NX)]

HIGH = lax.Precision.HIGH


def exchange(value, groups):
    return lax.all_to_all(value, "shard", 0, 0, axis_index_groups=groups, tiled=True)


def swap(value, bit):
    return lax.ppermute(value, "tensor", [(t, t ^ bit) for t in range(NT)])


def gram_of(matrix):
    return lax.dot_general(matrix, matrix, (((0,), (0,)), ((), ())), precision=HIGH)


def body(gradients, master_weights, first_moment, second_moment, old_basis, old_stats, owner_table):
    blocks = owner_table.shape[0]
    rows, width = gradients.shape[2:]
    rows_here = old_basis.shape[1]
    tensor = lax.axis_index("tensor")
    core = tensor % 2

    own = jnp.concatenate([old_basis, old_stats])
    other = swap(own, 2)
    pair = jnp.where(tensor < 2, jnp.stack([own, other]), jnp.stack([other, own]))
    mate = swap(pair, 1)
    whole = jnp.where(core == 0, jnp.stack([pair, mate], 1), jnp.stack([mate, pair], 1))
    whole_basis = whole[:, :, 0].reshape(width, width)
    whole_stats = whole[:, :, 1].reshape(width, width)

    places = jnp.arange(blocks, dtype=jnp.int32)
    wanted = (places % NYZ) * NX + places // NYZ
    source = jnp.sum(
        jnp.where(owner_table[None, :] == wanted[:, None], places[None, :], 0), axis=1
    )
    ordered = jnp.take(gradients[0], source, axis=0, mode="clip")
    parts = exchange(ordered.reshape(NX, NYZ, rows, width), X_GROUPS)
    partial = jnp.sum(parts, axis=0, dtype=jnp.float32)
    summed = jnp.sum(exchange(partial, YZ_GROUPS), axis=0)

    turned = jnp.dot(summed, whole_basis, precision=HIGH)
    first_new = momentum_decay * first_moment[0] + (1.0 - momentum_decay) * turned
    second_new = square_decay * second_moment[0] + (1.0 - square_decay) * turned * turned
    direction = first_new / jnp.sqrt(second_new)
    rotated_back = lax.dot_general(
        direction, whole_basis, (((1,), (1,)), ((), ())), precision=HIGH
    )
    weight_new = master_weights[0] - step_size * rotated_back

    column = exchange(jnp.broadcast_to(weight_new, (NYZ, rows, width)), YZ_GROUPS)
    gathered = exchange(jnp.broadcast_to(column, (NX, NYZ, rows, width)), X_GROUPS)
    gathered = gathered.reshape(blocks, rows, width)
    updated_weights = jnp.take(gathered, (owner_table % NX) * NYZ + owner_table // NX, axis=0, mode="clip")

    whole_grad = lax.all_gather(summed, "tensor", axis=0, tiled=True)
    stats_new = stats_decay * whole_stats + (1.0 - stats_decay) * gram_of(whole_grad)
    position = tensor * rows_here
    own_stats = lax.dynamic_slice_in_dim(stats_new, position, rows_here, 0)
    power = jnp.dot(stats_new, whole_basis, precision=HIGH)
    gram_matrix = gram_of(power)
    factor = start_gain / jnp.sqrt(jnp.trace(gram_matrix) + epsilon)
    current = power * factor
    gram_matrix = gram_matrix * (factor * factor)
    for sweep in range(NS_ITERS):
        if sweep > 0:
            gram_matrix = gram_of(current)
        if sweep + 1 < NS_ITERS:
            current = 1.5 * current - 0.5 * jnp.dot(current, gram_matrix, precision=HIGH)
        else:
            own_rows = lax.dynamic_slice_in_dim(current, position, rows_here, 0)
            current = 1.5 * own_rows - 0.5 * jnp.dot(own_rows, gram_matrix, precision=HIGH)
    return (updated_weights, first_new[None], second_new[None], current[None], own_stats[None])


def solution(mesh):
    return jax.shard_map(
        body,
        mesh=mesh,
        in_specs=(
            P("shard", None, "tensor", None),
            P("shard", "tensor", None),
            P("shard", "tensor", None),
            P("shard", "tensor", None),
            P("shard", "tensor", None),
            P("shard", "tensor", None),
            P(),
        ),
        out_specs=(
            P(None, "tensor", None),
            P("shard", "tensor", None),
            P("shard", "tensor", None),
            P("shard", "tensor", None),
            P("shard", "tensor", None),
        ),
        check_vma=False,
    )
```

time: 953 us -> 128 us (0.13)
  the two profiles are of different devices: /device:TPU:1 before, /device:TPU:48 now
where the time goes in v1:
time: 128 us; the launch traced here: 127 us
  waiting for transfers between devices  45.9 us (36%)
  starting transfers between devices  37.4 us (29%)
  blocking collectives  13.2 us (10%)
  local copies, waits for them, and re-layouts  12.5 us (10%)
  matrix products  9.41 us (7%)
  other arithmetic  7.19 us (6%)
  between operations  1.57 us (1%)
    all_to_all x4, waiting for transfers between devices, exchange(): lax.all_to_all(value, 'shard', 0, 0, axis_index_groups=groups, tiled=True)  41 us
    all_to_all x4, starting transfers between devices, exchange(): lax.all_to_all(value, 'shard', 0, 0, axis_index_groups=groups, tiled=True)  31.2 us
    all_gather x1, blocking collectives, body(): whole_grad = lax.all_gather(summed, 'tensor', axis=0, tiled=True)  13.2 us
    ppermute x2, starting transfers between devices, swap(): return lax.ppermute(value, 'tensor', [(t, t ^ bit) for t in range(NT)])  6.19 us
    ppermute x2, waiting for transfers between devices, swap(): return lax.ppermute(value, 'tensor', [(t, t ^ bit) for t in range(NT)])  4.95 us
    dot_general x4, matrix products, gram_of(): lax.dot_general(matrix, matrix, (((0,), (0,)), ((), ())), precision=HIGH)  4.32 us
    gather x1, local copies, waits for them, and re-layouts, body(): jnp.take(gathered, owner_table % NX * NYZ + owner_table // NX, axis=0, mo...  3.59 us
    broadcast_in_dim x1, local copies, waits for them, and re-layouts, body(): jnp.broadcast_to(column, (NX, NYZ, rows, width))  2.63 us
  transfers between devices with their start and end apart: 6, of which 4 were waited for; matrix products, arithmetic and copies ran while one was open for 14% of the time, Pallas kernels for 0%

profile of v1, /device:TPU:48, one launch (start us, length us, event | category | flops | bytes accessed | tf_op | source)
XLA Modules:
  0.0 127.2 jit_solution(12360427404006010425)
XLA Ops:
  0.6 0.0 copy-start
  0.6 1.1 constant_dynamic-update-slice_fusion.1
  1.7 1.0 constant_dynamic-update-slice_fusion
  2.7 4.3 %collective-permute-start = (f32[2,128,512]{2,1,0:T(8,128)S(1)}, f32[2,128,512]{2,1,0:T(8,128)S(1)}, u32[]{:S(2)}, u32[]{:S(2)}) collective-permute-start(f32[2,128,512]{2,1,0:T(8,128)S(1)} %constant_dynamic-update-slice_fusion), channel_id=1, source_target_pairs={{0,2},{1,3},{2,0},{3,1},{4,6},{5,7},{6,4},{7,5},{8,10},{9,11},{10,... | collective-permute-start | bytes 1572872 | tf_op jit(solution)/shard_map/ppermute | solution.py:29
  7.0 0.8 select_reduce_fusion.1
  7.8 0.0 copy-done
  7.8 1.7 %gather_fusion = bf16[128,8,512]{2,1,0:T(8,128)(2,1)} fusion(bf16[128,8,512]{2,1,0:T(8,128)(2,1)S(1)} %bitcast.51, s32[1024]{0:T(1024)S(1)} %pad_clamp_fusion.1), kind=kCustom, calls=%fused_computation | custom fusion | bytes 2097664 | tf_op jit(solution)/shard_map/jit(_take)/gather | solution.py:56
  9.5 0.0 copy-start.5
  9.5 4.4 %all-to-all-start = ((bf16[4,32,8,512]{3,2,1,0:T(8,128)(2,1)}), bf16[4,32,8,512]{3,2,1,0:T(8,128)(2,1)S(1)}, u32[]{:S(2)}, u32[]{:S(2)}) async-start(bf16[4,32,8,512]{3,2,1,0:T(8,128)(2,1)} %bitcast.3), calls=%async_computation | async-start | bytes 2097152 | tf_op jit(solution)/shard_map/all_to_all | solution.py:25
  13.9 4.9 %collective-permute-done = f32[2,128,512]{2,1,0:T(8,128)S(1)} collective-permute-done((f32[2,128,512]{2,1,0:T(8,128)S(1)}, f32[2,128,512]{2,1,0:T(8,128)S(1)}, u32[]{:S(2)}, u32[]{:S(2)}) %collective-permute-start) | collective-permute-done | bytes 524320 | tf_op jit(solution)/shard_map/ppermute | solution.py:29
  18.9 1.1 maximum_select_fusion.1
  20.0 1.9 %collective-permute-start.1 = (f32[2,2,128,512]{3,2,0,1:T(8,128)}, f32[2,2,128,512]{3,2,0,1:T(8,128)}, u32[]{:S(2)}, u32[]{:S(2)}) collective-permute-start(f32[2,2,128,512]{3,2,0,1:T(8,128)} %maximum_select_fusion.1), channel_id=1, source_target_pairs={{0,1},{1,0},{2,3},{3,2},{4,5},{5,4},{6,7},{7,6},{8,9},{9,8},{10,11... | collective-permute-start | bytes 3145736 | tf_op jit(solution)/shard_map/ppermute | solution.py:29
  21.9 0.0 copy-done.5
  21.9 6.8 %all-to-all-done = bf16[4,32,8,512]{3,2,1,0:T(8,128)(2,1)S(1)} async-done(((bf16[4,32,8,512]{3,2,1,0:T(8,128)(2,1)}), bf16[4,32,8,512]{3,2,1,0:T(8,128)(2,1)S(1)}, u32[]{:S(2)}, u32[]{:S(2)}) %all-to-all-start) | async-done | bytes 1048608 | tf_op jit(solution)/shard_map/all_to_all | solution.py:25
  28.7 0.9 convert_reduce_fusion
  29.7 14.8 %all-to-all-start.1 = ((f32[32,8,512]{2,1,0:T(8,128)}), f32[32,8,512]{2,1,0:T(8,128)}, u32[]{:S(2)}, u32[]{:S(2)}) async-start(f32[32,8,512]{2,1,0:T(8,128)} %convert_reduce_fusion), calls=%async_computation.1 | async-start | bytes 1048576 | tf_op jit(solution)/shard_map/all_to_all | solution.py:25
  44.5 0.3 pad_maximum_fusion
  44.8 0.2 copy_select_fusion
  45.0 0.0 collective-permute-done.1
  45.0 1.9 %maximum_select_fusion = f32[2,2,2,128,512]{4,3,1,0,2:T(8,128)S(1)} fusion(f32[2,1,2,128,512]{4,3,1,0,2:T(8,128)} %bitcast.8, f32[2,1,2,128,512]{4,3,1,0,2:T(8,128)S(1)} %copy_select_fusion, pred[]{:T(512)S(6)} %eq.28), kind=kLoop, calls=%fused_computation.2 | loop fusion | flops 1572864 | bytes 4194305 | tf_op jit(solution)/shard_map/jit(_where)/select_n | solution.py:47
  46.9 0.0 copy-start.2
  46.9 0.0 copy-start.3
  46.9 0.0 copy-start.4
  46.9 0.2 slice_multiply_fusion
  47.2 12.9 %all-to-all-done.1 = f32[32,8,512]{2,1,0:T(8,128)} async-done(((f32[32,8,512]{2,1,0:T(8,128)}), f32[32,8,512]{2,1,0:T(8,128)}, u32[]{:S(2)}, u32[]{:S(2)}) %all-to-all-start.1) | async-done | bytes 524320 | tf_op jit(solution)/shard_map/all_to_all | solution.py:25
  60.1 1.1 reduce_sum.39
  61.2 0.3 fusion.25
  61.5 0.0 copy-done.2
  61.5 0.0 copy-done.3
  61.5 0.0 copy-done.4
  61.5 0.5 fusion.4
  62.0 0.9 broadcast_in_dim.48
  62.9 7.5 %all-to-all-start.2 = ((f32[32,8,512]{2,1,0:T(8,128)}), f32[32,8,512]{2,1,0:T(8,128)}, u32[]{:S(2)}, u32[]{:S(2)}) async-start(f32[32,8,512]{2,1,0:T(8,128)} %broadcast_in_dim.48), calls=%async_computation.2 | async-start | bytes 1048576 | tf_op jit(solution)/shard_map/all_to_all | solution.py:25
  70.4 13.2 %all_gather.3 = f32[32,512]{1,0:T(8,128)S(1)} all-gather(f32[8,512]{1,0:T(8,128)S(1)} %reduce_sum.39), channel_id=1, replica_groups=mesh['shard'=128,'tensor'=4] {'tensor'}, dimensions={0}, use_global_device_ids=true | all-gather | bytes 81920 | tf_op jit(solution)/shard_map/all_gather | solution.py:75
  83.7 0.6 bitcast_add_fusion
  84.3 0.0 copy-start.1
  84.3 1.0 fusion.26
  85.3 1.6 %select_reduce_fusion = (f32[]{:T(128)}, f32[512,512]{1,0:T(8,128)S(1)}) fusion(f32[512,512]{1,0:T(8,128)S(1)} %fusion.26), kind=kOutput, calls=%fused_computation.22 | convolution fusion | flops 806092800 | bytes 2097156 | tf_op jit(solution)/shard_map/dot_general | solution.py:33
  87.0 0.0 copy-done.1
  87.7 1.7 %dynamic-slice_bitcast_fusion = f32[1,128,512]{2,1,0:T(8,128)} fusion(f32[512,512]{1,0:T(8,128)} %copy-done.1, s32[]{:T(128)S(6)} %select_n.86), kind=kLoop, calls=%fused_computation.26 | loop fusion | bytes 524292 | tf_op jit(solution)/shard_map/broadcast_in_dim | solution.py:92
  89.3 0.0 all-to-all-done.2
  89.3 2.6 %broadcast_in_dim.49 = f32[4,32,8,512]{3,2,1,0:T(8,128)} broadcast(f32[32,8,512]{2,1,0:T(8,128)} %all-to-all-done.2), dimensions={1,2,3} | broadcast | bytes 2621440 | tf_op jit(solution)/shard_map/broadcast_in_dim | solution.py:71
  92.0 4.5 %all-to-all-start.3 = ((f32[4,32,8,512]{3,2,1,0:T(8,128)}), f32[4,32,8,512]{3,2,1,0:T(8,128)}, u32[]{:S(2)}, u32[]{:S(2)}) async-start(f32[4,32,8,512]{3,2,1,0:T(8,128)} %broadcast_in_dim.49), calls=%async_computation.3 | async-start | bytes 4194304 | tf_op jit(solution)/shard_map/all_to_all | solution.py:25
  96.4 1.1 fusion.1
  97.5 1.0 fusion.27
  98.6 1.0 fusion
  99.6 1.0 fusion.28
  100.6 1.1 fusion.3
  101.7 0.6 fusion.14
  102.4 21.3 %all-to-all-done.3 = f32[4,32,8,512]{3,2,1,0:T(8,128)} async-done(((f32[4,32,8,512]{3,2,1,0:T(8,128)}), f32[4,32,8,512]{3,2,1,0:T(8,128)}, u32[]{:S(2)}, u32[]{:S(2)}) %all-to-all-start.3) | async-done | bytes 2097184 | tf_op jit(solution)/shard_map/all_to_all | solution.py:25
  123.6 3.6 %gather_fusion.1 = f32[128,8,512]{2,1,0:T(8,128)} fusion(f32[128,8,512]{2,1,0:T(8,128)} %bitcast.11, s32[1024]{0:T(1024)S(1)} %pad_clamp_fusion), kind=kCustom, calls=%fused_computation.1 | custom fusion | bytes 4194816 | tf_op jit(solution)/shard_map/jit(_take)/gather | solution.py:73
  (4 shorter events, 0.0 us)
Async XLA Ops:
  0.6 7.2 %copy-start = (bf16[1,128,8,512]{3,2,1,0:T(8,128)(2,1)S(1)}, bf16[1,128,8,512]{3,2,1,0:T(8,128)(2,1)}, u32[]{:S(2)}) copy-start(bf16[1,128,8,512]{3,2,1,0:T(8,128)(2,1)} %param.7) | copy-start | bytes 3145732
  2.7 16.2 %collective-permute-start = (f32[2,128,512]{2,1,0:T(8,128)S(1)}, f32[2,128,512]{2,1,0:T(8,128)S(1)}, u32[]{:S(2)}, u32[]{:S(2)}) collective-permute-start(f32[2,128,512]{2,1,0:T(8,128)S(1)} %constant_dynamic-update-slice_fusion), channel_id=1, source_target_pairs={{0,2},{1,3},{2,0},{3,1},{4,6},{5,7},{6,4},{7,5},{8,10},{9,11},{10,... | collective-permute-start | bytes 1572872 | tf_op jit(solution)/shard_map/ppermute | solution.py:29
  9.5 12.4 %copy-start.5 = (s32[128]{0:T(128)S(1)}, s32[128]{0:T(128)}, u32[]{:S(2)}) copy-start(s32[128]{0:T(128)} %param.13) | copy-start | bytes 1540
  9.5 19.2 %all-to-all-start = ((bf16[4,32,8,512]{3,2,1,0:T(8,128)(2,1)}), bf16[4,32,8,512]{3,2,1,0:T(8,128)(2,1)S(1)}, u32[]{:S(2)}, u32[]{:S(2)}) async-start(bf16[4,32,8,512]{3,2,1,0:T(8,128)(2,1)} %bitcast.3), calls=%async_computation | async-start | bytes 2097152 | tf_op jit(solution)/shard_map/all_to_all | solution.py:25
  20.0 25.0 %collective-permute-start.1 = (f32[2,2,128,512]{3,2,0,1:T(8,128)}, f32[2,2,128,512]{3,2,0,1:T(8,128)}, u32[]{:S(2)}, u32[]{:S(2)}) collective-permute-start(f32[2,2,128,512]{3,2,0,1:T(8,128)} %maximum_select_fusion.1), channel_id=1, source_target_pairs={{0,1},{1,0},{2,3},{3,2},{4,5},{5,4},{6,7},{7,6},{8,9},{9,8},{10,11... | collective-permute-start | bytes 3145736 | tf_op jit(solution)/shard_map/ppermute | solution.py:29
  29.7 30.4 %all-to-all-start.1 = ((f32[32,8,512]{2,1,0:T(8,128)}), f32[32,8,512]{2,1,0:T(8,128)}, u32[]{:S(2)}, u32[]{:S(2)}) async-start(f32[32,8,512]{2,1,0:T(8,128)} %convert_reduce_fusion), calls=%async_computation.1 | async-start | bytes 1048576 | tf_op jit(solution)/shard_map/all_to_all | solution.py:25
  46.9 14.6 %copy-start.2 = (f32[1,8,512]{2,1,0:T(8,128)S(1)}, f32[1,8,512]{2,1,0:T(8,128)}, u32[]{:S(2)}) copy-start(f32[1,8,512]{2,1,0:T(8,128)} %param.9) | copy-start | bytes 49156
  46.9 14.6 %copy-start.3 = (f32[1,8,512]{2,1,0:T(8,128)S(1)}, f32[1,8,512]{2,1,0:T(8,128)}, u32[]{:S(2)}) copy-start(f32[1,8,512]{2,1,0:T(8,128)} %param.10) | copy-start | bytes 49156
  46.9 14.6 %copy-start.4 = (f32[1,8,512]{2,1,0:T(8,128)S(1)}, f32[1,8,512]{2,1,0:T(8,128)}, u32[]{:S(2)}) copy-start(f32[1,8,512]{2,1,0:T(8,128)} %param.8) | copy-start | bytes 49156
  62.9 26.4 %all-to-all-start.2 = ((f32[32,8,512]{2,1,0:T(8,128)}), f32[32,8,512]{2,1,0:T(8,128)}, u32[]{:S(2)}, u32[]{:S(2)}) async-start(f32[32,8,512]{2,1,0:T(8,128)} %broadcast_in_dim.48), calls=%async_computation.2 | async-start | bytes 1048576 | tf_op jit(solution)/shard_map/all_to_all | solution.py:25
  84.3 2.6 %copy-start.1 = (f32[512,512]{1,0:T(8,128)}, f32[512,512]{1,0:T(8,128)S(1)}, u32[]{:S(2)}) copy-start(f32[512,512]{1,0:T(8,128)S(1)} %bitcast_add_fusion) | copy-start | bytes 3145732
  92.0 31.6 %all-to-all-start.3 = ((f32[4,32,8,512]{3,2,1,0:T(8,128)}), f32[4,32,8,512]{3,2,1,0:T(8,128)}, u32[]{:S(2)}, u32[]{:S(2)}) async-start(f32[4,32,8,512]{3,2,1,0:T(8,128)} %broadcast_in_dim.49), calls=%async_computation.3 | async-start | bytes 4194304 | tf_op jit(solution)/shard_map/all_to_all | solution.py:25

commit v2 on v1

--- a/solution.py
+++ b/solution.py
@@ -12,11 +12,25 @@
 start_gain = 1.7
 epsilon = 1e-06
 
-NY, NZ, NX = 8, 4, 4
-NYZ = NY * NZ
+NY_HI, NY_LO, NZ, NX = 4, 2, 4, 4
+NEAR, FAR = NY_LO * NX, NY_HI * NZ
 NT = 4
-X_GROUPS = [[yz * NX + x for x in range(NX)] for yz in range(NYZ)]
-YZ_GROUPS = [[yz * NX + x for yz in range(NYZ)] for x in range(NX)]
+
+
+def near_of(owner):
+    return owner // (NX * NZ) % NY_LO * NX + owner % NX
+
+
+def far_of(owner):
+    return owner // (NX * NZ * NY_LO) * NZ + owner // NX % NZ
+
+
+def owner_of(near, far):
+    return ((far // NZ * NY_LO + near // NX) * NZ + far % NZ) * NX + near % NX
+
+
+NEAR_GROUPS = [[owner_of(near, far) for near in range(NEAR)] for far in range(FAR)]
+FAR_GROUPS = [[owner_of(near, far) for far in range(FAR)] for near in range(NEAR)]
 
 HIGH = lax.Precision.HIGH
 
@@ -40,6 +54,17 @@
     tensor = lax.axis_index("tensor")
     core = tensor % 2
 
+    places = jnp.arange(blocks, dtype=jnp.int32)
+    wanted = owner_of(places // FAR, places % FAR)
+    source = jnp.sum(
+        jnp.where(owner_table[None, :] == wanted[:, None], places[None, :], 0), axis=1
+    )
+    ordered = jnp.take(gradients[0], source, axis=0, mode="clip")
+    ordered, old_basis, old_stats = lax.optimization_barrier((ordered, old_basis, old_stats))
+    parts = exchange(ordered.reshape(NEAR, FAR, rows, width), NEAR_GROUPS)
+    partial = jnp.sum(parts, axis=0, dtype=jnp.float32)
+    summed = jnp.sum(exchange(partial, FAR_GROUPS), axis=0)
+
     own = jnp.concatenate([old_basis, old_stats])
     other = swap(own, 2)
     pair = jnp.where(tensor < 2, jnp.stack([own, other]), jnp.stack([other, own]))
@@ -47,16 +72,6 @@
     whole = jnp.where(core == 0, jnp.stack([pair, mate], 1), jnp.stack([mate, pair], 1))
     whole_basis = whole[:, :, 0].reshape(width, width)
     whole_stats = whole[:, :, 1].reshape(width, width)
-
-    places = jnp.arange(blocks, dtype=jnp.int32)
-    wanted = (places % NYZ) * NX + places // NYZ
-    source = jnp.sum(
-        jnp.where(owner_table[None, :] == wanted[:, None], places[None, :], 0), axis=1
-    )
-    ordered = jnp.take(gradients[0], source, axis=0, mode="clip")
-    parts = exchange(ordered.reshape(NX, NYZ, rows, width), X_GROUPS)
-    partial = jnp.sum(parts, axis=0, dtype=jnp.float32)
-    summed = jnp.sum(exchange(partial, YZ_GROUPS), axis=0)
 
     turned = jnp.dot(summed, whole_basis, precision=HIGH)
     first_new = momentum_decay * first_moment[0] + (1.0 - momentum_decay) * turned
@@ -67,10 +82,22 @@
     )
     weight_new = master_weights[0] - step_size * rotated_back
 
-    column = exchange(jnp.broadcast_to(weight_new, (NYZ, rows, width)), YZ_GROUPS)
-    gathered = exchange(jnp.broadcast_to(column, (NX, NYZ, rows, width)), X_GROUPS)
-    gathered = gathered.reshape(blocks, rows, width)
-    updated_weights = jnp.take(gathered, (owner_table % NX) * NYZ + owner_table // NX, axis=0, mode="clip")
+    copies = jnp.broadcast_to(weight_new, (FAR, rows, width))
+    copies, summed = lax.optimization_barrier((copies, summed))
+    column = exchange(copies, FAR_GROUPS)
+    largest = jnp.maximum(jnp.max(jnp.abs(column)), 2.0**-100)
+    exponent = jnp.ceil(jnp.log2(largest))
+    coded = (column * jnp.exp2(14.0 - exponent)).astype(jnp.float16)
+    label = jnp.broadcast_to(exponent.astype(jnp.float16), (1, rows, width))
+    coded = jnp.broadcast_to(jnp.concatenate([coded, label]), (NEAR, FAR + 1, rows, width))
+    gathered = exchange(coded, NEAR_GROUPS)
+    scales = jnp.exp2(gathered[:, FAR, 0, 0].astype(jnp.float32) - 14.0)
+    near = near_of(owner_table)
+    wide = jnp.take(
+        gathered.reshape(NEAR * (FAR + 1), rows, width), near * (FAR + 1) + far_of(owner_table), axis=0, mode="clip"
+    )
+    scale = jnp.sum(jnp.where(near[:, None] == jnp.arange(NEAR)[None, :], scales[None, :], 0.0), axis=1)
+    updated_weights = wide.astype(jnp.float32) * scale[:, None, None]
 
     whole_grad = lax.all_gather(summed, "tensor", axis=0, tiled=True)
     stats_new = stats_decay * whole_stats + (1.0 - stats_decay) * gram_of(whole_grad)

time: 128 us -> 115 us (0.90)
  the two profiles are of different devices: /device:TPU:48 before, /device:TPU:1 now
where the time goes in v2:
time: 115 us
  starting transfers between devices  43.2 us (38%)
  waiting for transfers between devices  30.9 us (27%)
  matrix products  11.6 us (10%)
  other arithmetic  11.2 us (10%)
  local copies, waits for them, and re-layouts  7.73 us (7%)
  blocking collectives  7.66 us (7%)
  between operations  2.39 us (2%)
    all_to_all x4, starting transfers between devices, exchange(): lax.all_to_all(value, 'shard', 0, 0, axis_index_groups=groups, tiled=True)  32.8 us
    all_to_all x4, waiting for transfers between devices, exchange(): lax.all_to_all(value, 'shard', 0, 0, axis_index_groups=groups, tiled=True)  22.6 us
    ppermute x2, starting transfers between devices, swap(): return lax.ppermute(value, 'tensor', [(t, t ^ bit) for t in range(NT)])  10.4 us
    ppermute x2, waiting for transfers between devices, swap(): return lax.ppermute(value, 'tensor', [(t, t ^ bit) for t in range(NT)])  8.37 us
    all_gather x1, blocking collectives, body(): whole_grad = lax.all_gather(summed, 'tensor', axis=0, tiled=True)  7.66 us
    dot_general x4, matrix products, gram_of(): lax.dot_general(matrix, matrix, (((0,), (0,)), ((), ())), precision=HIGH)  5.29 us
    dot_general x2, matrix products, body(): jnp.dot(current, gram_matrix, precision=HIGH)  3.29 us
  transfers between devices with their start and end apart: 6, of which 4 were waited for; matrix products, arithmetic and copies ran while one was open for 18% of the time, Pallas kernels for 0%

profile of v2, /device:TPU:1, one launch (start us, length us, event | category | flops | bytes accessed | tf_op | source)
XLA Modules:
  0.0 114.7 jit_solution(6967155064957867471)
XLA Ops:
  0.6 0.0 copy-start
  0.7 0.9 select_reduce_fusion.1
  1.6 0.3 copy-done
  1.9 0.0 copy-start.4
  1.9 0.0 copy-start.5
  1.9 1.7 %gather_fusion = bf16[128,8,512]{2,1,0:T(8,128)(2,1)} fusion(bf16[128,8,512]{2,1,0:T(8,128)(2,1)S(1)} %bitcast.53, s32[1024]{0:T(1024)S(1)} %pad_clamp_fusion.1), kind=kCustom, calls=%fused_computation | custom fusion | bytes 2097664 | tf_op jit(solution)/shard_map/jit(_take)/gather | solution.py:62
  3.6 5.9 %all-to-all-start = ((bf16[8,16,8,512]{3,2,1,0:T(8,128)(2,1)}), bf16[8,16,8,512]{3,2,1,0:T(8,128)(2,1)}, u32[]{:S(2)}, u32[]{:S(2)}) async-start(bf16[8,16,8,512]{3,2,1,0:T(8,128)(2,1)} %bitcast.3), calls=%async_computation | async-start | bytes 2097152 | tf_op jit(solution)/shard_map/all_to_all | solution.py:39
  9.4 0.0 copy-done.4
  9.4 0.0 copy-start.9
  9.5 0.0 copy-done.5
  9.5 0.0 copy-start.2
  9.5 4.0 %collective-permute-start = (f32[2,128,512]{2,1,0:T(8,128)S(1)}, f32[2,128,512]{2,1,0:T(8,128)S(1)}, u32[]{:S(2)}, u32[]{:S(2)}) collective-permute-start(f32[2,128,512]{2,1,0:T(8,128)S(1)} %constant_dynamic-update-slice_fusion), channel_id=1, source_target_pairs={{0,2},{1,3},{2,0},{3,1},{4,6},{5,7},{6,4},{7,5},{8,10},{9,11},{10,... | collective-permute-start | bytes 1572872 | tf_op jit(solution)/shard_map/ppermute | solution.py:43
  13.5 8.4 %collective-permute-done = f32[2,128,512]{2,1,0:T(8,128)S(1)} collective-permute-done((f32[2,128,512]{2,1,0:T(8,128)S(1)}, f32[2,128,512]{2,1,0:T(8,128)S(1)}, u32[]{:S(2)}, u32[]{:S(2)}) %collective-permute-start) | collective-permute-done | bytes 524320 | tf_op jit(solution)/shard_map/ppermute | solution.py:43
  21.9 0.0 copy-start.3
  21.9 1.1 maximum_select_fusion.1
  23.0 6.4 %collective-permute-start.1 = (f32[2,2,128,512]{3,2,0,1:T(8,128)}, f32[2,2,128,512]{3,2,0,1:T(8,128)}, u32[]{:S(2)}, u32[]{:S(2)}) collective-permute-start(f32[2,2,128,512]{3,2,0,1:T(8,128)} %maximum_select_fusion.1), channel_id=1, source_target_pairs={{0,1},{1,0},{2,3},{3,2},{4,5},{5,4},{6,7},{7,6},{8,9},{9,8},{10,11... | collective-permute-start | bytes 3145736 | tf_op jit(solution)/shard_map/ppermute | solution.py:43
  29.4 0.0 copy-done.9
  29.5 0.0 copy-done.2
  29.5 0.0 copy-done.3
  29.5 1.8 %pad_maximum_fusion = (f32[2,1,2,128,512]{4,3,2,1,0:T(8,128)S(1)}, f32[2,1,2,128,512]{4,3,2,1,0:T(8,128)S(1)}) fusion(f32[1,1,2,128,512]{4,3,2,1,0:T(8,128)} %bitcast.61, f32[1,1,2,128,512]{4,3,2,1,0:T(8,128)} %bitcast.59), kind=kLoop, calls=%fused_computation.16 | loop fusion | flops 524288 | bytes 3145728 | tf_op jit(solution)/shard_map/stack | solution.py:70
  31.3 0.0 all-to-all-done
  31.3 2.1 %convert_reduce_fusion = f32[16,8,512]{2,1,0:T(8,128)} fusion(bf16[8,16,8,512]{3,2,1,0:T(8,128)(2,1)} %all-to-all-done), kind=kLoop, calls=%fused_computation.4 | loop fusion | flops 983040 | bytes 1310720 | tf_op jit(solution)/shard_map/reduce_sum | solution.py:65
  33.4 14.0 %all-to-all-start.1 = ((f32[16,8,512]{2,1,0:T(8,128)}), f32[16,8,512]{2,1,0:T(8,128)S(1)}, u32[]{:S(2)}, u32[]{:S(2)}) async-start(f32[16,8,512]{2,1,0:T(8,128)} %convert_reduce_fusion), calls=%async_computation.1 | async-start | bytes 524288 | tf_op jit(solution)/shard_map/all_to_all | solution.py:39
  47.4 0.2 copy_select_fusion
  47.6 0.0 collective-permute-done.1
  47.6 1.9 %maximum_select_fusion = f32[2,2,2,128,512]{4,3,1,0,2:T(8,128)S(1)} fusion(f32[2,1,2,128,512]{4,3,1,0,2:T(8,128)} %bitcast.8, f32[2,1,2,128,512]{4,3,1,0,2:T(8,128)S(1)} %copy_select_fusion, pred[]{:T(512)S(6)} %eq.45), kind=kLoop, calls=%fused_computation.2 | loop fusion | flops 1572864 | bytes 4194305 | tf_op jit(solution)/shard_map/jit(_where)/select_n | solution.py:72
  49.5 0.0 copy-start.6
  49.5 0.0 copy-start.7
  49.5 0.0 copy-start.8
  49.6 0.2 slice_multiply_fusion
  49.8 9.8 %all-to-all-done.1 = f32[16,8,512]{2,1,0:T(8,128)S(1)} async-done(((f32[16,8,512]{2,1,0:T(8,128)}), f32[16,8,512]{2,1,0:T(8,128)S(1)}, u32[]{:S(2)}, u32[]{:S(2)}) %all-to-all-start.1) | async-done | bytes 262176 | tf_op jit(solution)/shard_map/all_to_all | solution.py:39
  59.5 0.4 fusion.30
  59.9 0.0 copy-done.6
  59.9 0.0 copy-done.7
  59.9 0.0 copy-done.8
  59.9 0.5 fusion.4
  60.4 0.7 broadcast_in_dim.65
  61.2 7.7 %all_gather.3 = f32[32,512]{1,0:T(8,128)S(1)} all-gather(f32[8,512]{1,0:T(8,128)S(1)} %reduce_sum.48), channel_id=1, replica_groups=mesh['shard'=128,'tensor'=4] {'tensor'}, dimensions={0}, use_global_device_ids=true | all-gather | bytes 81920 | tf_op jit(solution)/shard_map/all_gather | solution.py:102
  68.8 4.6 %all-to-all-start.2 = ((f32[16,8,512]{2,1,0:T(8,128)}), f32[16,8,512]{2,1,0:T(8,128)S(1)}, u32[]{:S(2)}, u32[]{:S(2)}) async-start(f32[16,8,512]{2,1,0:T(8,128)} %broadcast_in_dim.65), calls=%async_computation.2 | async-start | bytes 524288 | tf_op jit(solution)/shard_map/all_to_all | solution.py:39
  73.5 0.6 bitcast_add_fusion
  74.2 0.0 copy-start.1
  74.2 1.0 copy-done.1
  75.2 1.0 fusion.31
  76.2 9.3 %all-to-all-done.2 = f32[16,8,512]{2,1,0:T(8,128)S(1)} async-done(((f32[16,8,512]{2,1,0:T(8,128)}), f32[16,8,512]{2,1,0:T(8,128)S(1)}, u32[]{:S(2)}, u32[]{:S(2)}) %all-to-all-start.2) | async-done | bytes 262176 | tf_op jit(solution)/shard_map/all_to_all | solution.py:39
  85.5 0.6 abs_reduce_fusion
  86.9 1.1 broadcast_in_dim.66
  88.0 8.3 %all-to-all-start.3 = ((f16[8,17,8,512]{3,2,1,0:T(8,128)(2,1)}), f16[8,17,8,512]{3,2,1,0:T(8,128)(2,1)S(1)}, u32[]{:S(2)}, u32[]{:S(2)}) async-start(f16[8,17,8,512]{3,2,1,0:T(8,128)(2,1)} %broadcast_in_dim.66), calls=%async_computation.3 | async-start | bytes 2228224 | tf_op jit(solution)/shard_map/all_to_all | solution.py:39
  96.3 2.6 %select_reduce_fusion = (f32[]{:T(128)}, f32[512,512]{1,0:T(8,128)}) fusion(f32[512,512]{1,0:T(8,128)S(1)} %fusion.31), kind=kOutput, calls=%fused_computation.23 | convolution fusion | flops 806092800 | bytes 2097156 | tf_op jit(solution)/shard_map/dot_general | solution.py:47
  99.6 1.7 %dynamic-slice_bitcast_fusion = f32[1,128,512]{2,1,0:T(8,128)} fusion(f32[512,512]{1,0:T(8,128)} %copy-done.1, s32[]{:T(128)S(6)} %select_n.143), kind=kLoop, calls=%fused_computation.27 | loop fusion | bytes 524292 | tf_op jit(solution)/shard_map/broadcast_in_dim | solution.py:119
  101.3 2.3 %fusion.1 = f32[512,512]{1,0:T(8,128)S(1)} fusion(f32[512,512]{1,0:T(8,128)} %get-tuple-element.24, f32[512,512]{1,0:T(8,128)S(1)} %fusion.31, f32[]{:T(128)S(6)} %mul.171, f32[]{:T(128)S(6)} %div.78), kind=kOutput, calls=%fused_computation.8 | convolution fusion | flops 806879232 | bytes 3145736 | tf_op jit(solution)/shard_map/dot_general | solution.py:115
  103.6 1.0 fusion.32
  104.6 1.0 fusion
  105.6 1.0 fusion.33
  106.7 1.1 fusion.3
  107.8 0.6 fusion.14
  108.4 3.6 %all-to-all-done.3 = f16[8,17,8,512]{3,2,1,0:T(8,128)(2,1)S(1)} async-done(((f16[8,17,8,512]{3,2,1,0:T(8,128)(2,1)}), f16[8,17,8,512]{3,2,1,0:T(8,128)(2,1)S(1)}, u32[]{:S(2)}, u32[]{:S(2)}) %all-to-all-start.3) | async-done | bytes 1114144 | tf_op jit(solution)/shard_map/all_to_all | solution.py:39
  112.0 0.1 copy.25
  112.1 1.0 gather_fusion.1
  113.1 0.1 select_reduce_fusion.2
  113.2 1.5 %convert_multiply_fusion = f32[128,8,512]{2,1,0:T(8,128)} fusion(f16[128,8,512]{2,1,0:T(8,128)(2,1)S(1)} %gather_fusion.1, f32[128]{0:T(128)S(1)} %select_reduce_fusion.2), kind=kLoop, calls=%fused_computation.3 | loop fusion | flops 1048576 | bytes 3146240 | tf_op jit(solution)/shard_map/mul | solution.py:100
  (11 shorter events, 0.2 us)
Async XLA Ops:
  0.6 1.2 %copy-start = (bf16[1,128,8,512]{3,2,1,0:T(8,128)(2,1)S(1)}, bf16[1,128,8,512]{3,2,1,0:T(8,128)(2,1)}, u32[]{:S(2)}) copy-start(bf16[1,128,8,512]{3,2,1,0:T(8,128)(2,1)} %param.7) | copy-start | bytes 3145732
  1.9 7.5 %copy-start.4 = (f32[1,128,512]{2,1,0:T(8,128)S(1)}, f32[1,128,512]{2,1,0:T(8,128)}, u32[]{:S(2)}) copy-start(f32[1,128,512]{2,1,0:T(8,128)} %param.11) | copy-start | bytes 786436
  1.9 7.6 %copy-start.5 = (f32[1,128,512]{2,1,0:T(8,128)S(1)}, f32[1,128,512]{2,1,0:T(8,128)}, u32[]{:S(2)}) copy-start(f32[1,128,512]{2,1,0:T(8,128)} %param.12) | copy-start | bytes 786436
  3.6 27.8 %all-to-all-start = ((bf16[8,16,8,512]{3,2,1,0:T(8,128)(2,1)}), bf16[8,16,8,512]{3,2,1,0:T(8,128)(2,1)}, u32[]{:S(2)}, u32[]{:S(2)}) async-start(bf16[8,16,8,512]{3,2,1,0:T(8,128)(2,1)} %bitcast.3), calls=%async_computation | async-start | bytes 2097152 | tf_op jit(solution)/shard_map/all_to_all | solution.py:39
  9.4 20.0 %copy-start.9 = (s32[128]{0:T(128)S(1)}, s32[128]{0:T(128)}, u32[]{:S(2)}) copy-start(s32[128]{0:T(128)} %param.13) | copy-start | bytes 1540
  9.5 20.0 %copy-start.2 = (f32[2,128,512]{2,1,0:T(8,128)}, f32[2,128,512]{2,1,0:T(8,128)S(1)}, u32[]{:S(2)}) copy-start(f32[2,128,512]{2,1,0:T(8,128)S(1)} %constant_dynamic-update-slice_fusion) | copy-start | bytes 1572868
  9.5 12.4 %collective-permute-start = (f32[2,128,512]{2,1,0:T(8,128)S(1)}, f32[2,128,512]{2,1,0:T(8,128)S(1)}, u32[]{:S(2)}, u32[]{:S(2)}) collective-permute-start(f32[2,128,512]{2,1,0:T(8,128)S(1)} %constant_dynamic-update-slice_fusion), channel_id=1, source_target_pairs={{0,2},{1,3},{2,0},{3,1},{4,6},{5,7},{6,4},{7,5},{8,10},{9,11},{10,... | collective-permute-start | bytes 1572872 | tf_op jit(solution)/shard_map/ppermute | solution.py:43
  21.9 7.6 %copy-start.3 = (f32[2,128,512]{2,1,0:T(8,128)}, f32[2,128,512]{2,1,0:T(8,128)S(1)}, u32[]{:S(2)}) copy-start(f32[2,128,512]{2,1,0:T(8,128)S(1)} %collective-permute-done) | copy-start | bytes 1572868
  23.0 24.6 %collective-permute-start.1 = (f32[2,2,128,512]{3,2,0,1:T(8,128)}, f32[2,2,128,512]{3,2,0,1:T(8,128)}, u32[]{:S(2)}, u32[]{:S(2)}) collective-permute-start(f32[2,2,128,512]{3,2,0,1:T(8,128)} %maximum_select_fusion.1), channel_id=1, source_target_pairs={{0,1},{1,0},{2,3},{3,2},{4,5},{5,4},{6,7},{7,6},{8,9},{9,8},{10,11... | collective-permute-start | bytes 3145736 | tf_op jit(solution)/shard_map/ppermute | solution.py:43
  33.4 26.1 %all-to-all-start.1 = ((f32[16,8,512]{2,1,0:T(8,128)}), f32[16,8,512]{2,1,0:T(8,128)S(1)}, u32[]{:S(2)}, u32[]{:S(2)}) async-start(f32[16,8,512]{2,1,0:T(8,128)} %convert_reduce_fusion), calls=%async_computation.1 | async-start | bytes 524288 | tf_op jit(solution)/shard_map/all_to_all | solution.py:39
  49.5 10.4 %copy-start.6 = (f32[1,8,512]{2,1,0:T(8,128)S(1)}, f32[1,8,512]{2,1,0:T(8,128)}, u32[]{:S(2)}) copy-start(f32[1,8,512]{2,1,0:T(8,128)} %param.9) | copy-start | bytes 49156
  49.5 10.4 %copy-start.7 = (f32[1,8,512]{2,1,0:T(8,128)S(1)}, f32[1,8,512]{2,1,0:T(8,128)}, u32[]{:S(2)}) copy-start(f32[1,8,512]{2,1,0:T(8,128)} %param.10) | copy-start | bytes 49156
  49.5 10.4 %copy-start.8 = (f32[1,8,512]{2,1,0:T(8,128)S(1)}, f32[1,8,512]{2,1,0:T(8,128)}, u32[]{:S(2)}) copy-start(f32[1,8,512]{2,1,0:T(8,128)} %param.8) | copy-start | bytes 49156
  68.8 16.6 %all-to-all-start.2 = ((f32[16,8,512]{2,1,0:T(8,128)}), f32[16,8,512]{2,1,0:T(8,128)S(1)}, u32[]{:S(2)}, u32[]{:S(2)}) async-start(f32[16,8,512]{2,1,0:T(8,128)} %broadcast_in_dim.65), calls=%async_computation.2 | async-start | bytes 524288 | tf_op jit(solution)/shard_map/all_to_all | solution.py:39
  74.2 1.0 copy-start.1
  88.0 24.0 %all-to-all-start.3 = ((f16[8,17,8,512]{3,2,1,0:T(8,128)(2,1)}), f16[8,17,8,512]{3,2,1,0:T(8,128)(2,1)S(1)}, u32[]{:S(2)}, u32[]{:S(2)}) async-start(f16[8,17,8,512]{3,2,1,0:T(8,128)(2,1)} %broadcast_in_dim.66), calls=%async_computation.3 | async-start | bytes 2228224 | tf_op jit(solution)/shard_map/all_to_all | solution.py:39

commit v3 on v2

--- a/solution.py
+++ b/solution.py
@@ -2,6 +2,7 @@
 import jax.numpy as jnp
 from jax import lax
 from jax.sharding import PartitionSpec as P
+
 
 NS_ITERS = 3
 
@@ -47,7 +48,7 @@
     return lax.dot_general(matrix, matrix, (((0,), (0,)), ((), ())), precision=HIGH)
 
 
-def body(gradients, master_weights, first_moment, second_moment, old_basis, old_stats, owner_table):
+def step(gradients, master_weights, first_moment, second_moment, old_basis, old_stats, owner_table):
     blocks = owner_table.shape[0]
     rows, width = gradients.shape[2:]
     rows_here = old_basis.shape[1]
@@ -63,7 +64,8 @@
     ordered, old_basis, old_stats = lax.optimization_barrier((ordered, old_basis, old_stats))
     parts = exchange(ordered.reshape(NEAR, FAR, rows, width), NEAR_GROUPS)
     partial = jnp.sum(parts, axis=0, dtype=jnp.float32)
-    summed = jnp.sum(exchange(partial, FAR_GROUPS), axis=0)
+    parts = exchange(partial, FAR_GROUPS)
+    summed = jnp.sum(parts, axis=0)
 
     own = jnp.concatenate([old_basis, old_stats])
     other = swap(own, 2)
@@ -71,7 +73,7 @@
     mate = swap(pair, 1)
     whole = jnp.where(core == 0, jnp.stack([pair, mate], 1), jnp.stack([mate, pair], 1))
     whole_basis = whole[:, :, 0].reshape(width, width)
-    whole_stats = whole[:, :, 1].reshape(width, width)
+    decayed_stats = stats_decay * whole[:, :, 1].reshape(width, width)
 
     turned = jnp.dot(summed, whole_basis, precision=HIGH)
     first_new = momentum_decay * first_moment[0] + (1.0 - momentum_decay) * turned
@@ -100,7 +102,7 @@
     updated_weights = wide.astype(jnp.float32) * scale[:, None, None]
 
     whole_grad = lax.all_gather(summed, "tensor", axis=0, tiled=True)
-    stats_new = stats_decay * whole_stats + (1.0 - stats_decay) * gram_of(whole_grad)
+    stats_new = decayed_stats + (1.0 - stats_decay) * gram_of(whole_grad)
     position = tensor * rows_here
     own_stats = lax.dynamic_slice_in_dim(stats_new, position, rows_here, 0)
     power = jnp.dot(stats_new, whole_basis, precision=HIGH)
@@ -121,7 +123,7 @@
 
 def solution(mesh):
     return jax.shard_map(
-        body,
+        step,
         mesh=mesh,
         in_specs=(
             P("shard", None, "tensor", None),

time: 115 us -> 115 us (level)
  no operation moved by 1% of the time
where the time goes in v3:
time: 115 us
  starting transfers between devices  43.2 us (38%)
  waiting for transfers between devices  30.9 us (27%)
  matrix products  11.6 us (10%)
  other arithmetic  11.2 us (10%)
  local copies, waits for them, and re-layouts  7.73 us (7%)
  blocking collectives  7.66 us (7%)
  between operations  2.39 us (2%)
    all_to_all x4, starting transfers between devices, exchange(): lax.all_to_all(value, 'shard', 0, 0, axis_index_groups=groups, tiled=True)  32.8 us
    all_to_all x4, waiting for transfers between devices, exchange(): lax.all_to_all(value, 'shard', 0, 0, axis_index_groups=groups, tiled=True)  22.6 us
    ppermute x2, starting transfers between devices, swap(): return lax.ppermute(value, 'tensor', [(t, t ^ bit) for t in range(NT)])  10.4 us
    ppermute x2, waiting for transfers between devices, swap(): return lax.ppermute(value, 'tensor', [(t, t ^ bit) for t in range(NT)])  8.37 us
    all_gather x1, blocking collectives, step(): whole_grad = lax.all_gather(summed, 'tensor', axis=0, tiled=True)  7.66 us
    dot_general x4, matrix products, gram_of(): lax.dot_general(matrix, matrix, (((0,), (0,)), ((), ())), precision=HIGH)  5.29 us
    dot_general x2, matrix products, step(): jnp.dot(current, gram_matrix, precision=HIGH)  3.29 us
  transfers between devices with their start and end apart: 6, of which 4 were waited for; matrix products, arithmetic and copies ran while one was open for 18% of the time, Pallas kernels for 0%

profile of v3, /device:TPU:1, one launch (start us, length us, event | category | flops | bytes accessed | tf_op | source)
XLA Modules:
  0.0 114.7 jit_solution(6967155064957867471)
XLA Ops:
  0.6 0.0 copy-start
  0.7 0.9 select_reduce_fusion.1
  1.6 0.3 copy-done
  1.9 0.0 copy-start.4
  1.9 0.0 copy-start.5
  1.9 1.7 %gather_fusion = bf16[128,8,512]{2,1,0:T(8,128)(2,1)} fusion(bf16[128,8,512]{2,1,0:T(8,128)(2,1)S(1)} %bitcast.53, s32[1024]{0:T(1024)S(1)} %pad_clamp_fusion.1), kind=kCustom, calls=%fused_computation | custom fusion | bytes 2097664 | tf_op jit(solution)/shard_map/jit(_take)/gather | solution.py:63
  3.6 5.9 %all-to-all-start = ((bf16[8,16,8,512]{3,2,1,0:T(8,128)(2,1)}), bf16[8,16,8,512]{3,2,1,0:T(8,128)(2,1)}, u32[]{:S(2)}, u32[]{:S(2)}) async-start(bf16[8,16,8,512]{3,2,1,0:T(8,128)(2,1)} %bitcast.3), calls=%async_computation | async-start | bytes 2097152 | tf_op jit(solution)/shard_map/all_to_all | solution.py:40
  9.4 0.0 copy-done.4
  9.4 0.0 copy-start.9
  9.5 0.0 copy-done.5
  9.5 0.0 copy-start.2
  9.5 4.0 %collective-permute-start = (f32[2,128,512]{2,1,0:T(8,128)S(1)}, f32[2,128,512]{2,1,0:T(8,128)S(1)}, u32[]{:S(2)}, u32[]{:S(2)}) collective-permute-start(f32[2,128,512]{2,1,0:T(8,128)S(1)} %constant_dynamic-update-slice_fusion), channel_id=1, source_target_pairs={{0,2},{1,3},{2,0},{3,1},{4,6},{5,7},{6,4},{7,5},{8,10},{9,11},{10,... | collective-permute-start | bytes 1572872 | tf_op jit(solution)/shard_map/ppermute | solution.py:44
  13.5 8.4 %collective-permute-done = f32[2,128,512]{2,1,0:T(8,128)S(1)} collective-permute-done((f32[2,128,512]{2,1,0:T(8,128)S(1)}, f32[2,128,512]{2,1,0:T(8,128)S(1)}, u32[]{:S(2)}, u32[]{:S(2)}) %collective-permute-start) | collective-permute-done | bytes 524320 | tf_op jit(solution)/shard_map/ppermute | solution.py:44
  21.9 0.0 copy-start.3
  21.9 1.1 maximum_select_fusion.1
  23.0 6.4 %collective-permute-start.1 = (f32[2,2,128,512]{3,2,0,1:T(8,128)}, f32[2,2,128,512]{3,2,0,1:T(8,128)}, u32[]{:S(2)}, u32[]{:S(2)}) collective-permute-start(f32[2,2,128,512]{3,2,0,1:T(8,128)} %maximum_select_fusion.1), channel_id=1, source_target_pairs={{0,1},{1,0},{2,3},{3,2},{4,5},{5,4},{6,7},{7,6},{8,9},{9,8},{10,11... | collective-permute-start | bytes 3145736 | tf_op jit(solution)/shard_map/ppermute | solution.py:44
  29.4 0.0 copy-done.9
  29.5 0.0 copy-done.2
  29.5 0.0 copy-done.3
  29.5 1.8 %pad_maximum_fusion = (f32[2,1,2,128,512]{4,3,2,1,0:T(8,128)S(1)}, f32[2,1,2,128,512]{4,3,2,1,0:T(8,128)S(1)}) fusion(f32[1,1,2,128,512]{4,3,2,1,0:T(8,128)} %bitcast.61, f32[1,1,2,128,512]{4,3,2,1,0:T(8,128)} %bitcast.59), kind=kLoop, calls=%fused_computation.16 | loop fusion | flops 524288 | bytes 3145728 | tf_op jit(solution)/shard_map/stack | solution.py:72
  31.3 0.0 all-to-all-done
  31.3 2.1 %convert_reduce_fusion = f32[16,8,512]{2,1,0:T(8,128)} fusion(bf16[8,16,8,512]{3,2,1,0:T(8,128)(2,1)} %all-to-all-done), kind=kLoop, calls=%fused_computation.4 | loop fusion | flops 983040 | bytes 1310720 | tf_op jit(solution)/shard_map/reduce_sum | solution.py:66
  33.4 14.0 %all-to-all-start.1 = ((f32[16,8,512]{2,1,0:T(8,128)}), f32[16,8,512]{2,1,0:T(8,128)S(1)}, u32[]{:S(2)}, u32[]{:S(2)}) async-start(f32[16,8,512]{2,1,0:T(8,128)} %convert_reduce_fusion), calls=%async_computation.1 | async-start | bytes 524288 | tf_op jit(solution)/shard_map/all_to_all | solution.py:40
  47.4 0.2 copy_select_fusion
  47.6 0.0 collective-permute-done.1
  47.6 1.9 %maximum_select_fusion = f32[2,2,2,128,512]{4,3,1,0,2:T(8,128)S(1)} fusion(f32[2,1,2,128,512]{4,3,1,0,2:T(8,128)} %bitcast.8, f32[2,1,2,128,512]{4,3,1,0,2:T(8,128)S(1)} %copy_select_fusion, pred[]{:T(512)S(6)} %eq.45), kind=kLoop, calls=%fused_computation.2 | loop fusion | flops 1572864 | bytes 4194305 | tf_op jit(solution)/shard_map/jit(_where)/select_n | solution.py:74
  49.5 0.0 copy-start.6
  49.5 0.0 copy-start.7
  49.5 0.0 copy-start.8
  49.6 0.2 slice_multiply_fusion
  49.8 9.8 %all-to-all-done.1 = f32[16,8,512]{2,1,0:T(8,128)S(1)} async-done(((f32[16,8,512]{2,1,0:T(8,128)}), f32[16,8,512]{2,1,0:T(8,128)S(1)}, u32[]{:S(2)}, u32[]{:S(2)}) %all-to-all-start.1) | async-done | bytes 262176 | tf_op jit(solution)/shard_map/all_to_all | solution.py:40
  59.5 0.4 fusion.30
  59.9 0.0 copy-done.6
  59.9 0.0 copy-done.7
  59.9 0.0 copy-done.8
  59.9 0.5 fusion.4
  60.4 0.7 broadcast_in_dim.65
  61.2 7.7 %all_gather.3 = f32[32,512]{1,0:T(8,128)S(1)} all-gather(f32[8,512]{1,0:T(8,128)S(1)} %reduce_sum.48), channel_id=1, replica_groups=mesh['shard'=128,'tensor'=4] {'tensor'}, dimensions={0}, use_global_device_ids=true | all-gather | bytes 81920 | tf_op jit(solution)/shard_map/all_gather | solution.py:104
  68.8 4.6 %all-to-all-start.2 = ((f32[16,8,512]{2,1,0:T(8,128)}), f32[16,8,512]{2,1,0:T(8,128)S(1)}, u32[]{:S(2)}, u32[]{:S(2)}) async-start(f32[16,8,512]{2,1,0:T(8,128)} %broadcast_in_dim.65), calls=%async_computation.2 | async-start | bytes 524288 | tf_op jit(solution)/shard_map/all_to_all | solution.py:40
  73.5 0.6 bitcast_add_fusion
  74.2 0.0 copy-start.1
  74.2 1.0 copy-done.1
  75.2 1.0 fusion.31
  76.2 9.3 %all-to-all-done.2 = f32[16,8,512]{2,1,0:T(8,128)S(1)} async-done(((f32[16,8,512]{2,1,0:T(8,128)}), f32[16,8,512]{2,1,0:T(8,128)S(1)}, u32[]{:S(2)}, u32[]{:S(2)}) %all-to-all-start.2) | async-done | bytes 262176 | tf_op jit(solution)/shard_map/all_to_all | solution.py:40
  85.5 0.6 abs_reduce_fusion
  86.9 1.1 broadcast_in_dim.66
  88.0 8.3 %all-to-all-start.3 = ((f16[8,17,8,512]{3,2,1,0:T(8,128)(2,1)}), f16[8,17,8,512]{3,2,1,0:T(8,128)(2,1)S(1)}, u32[]{:S(2)}, u32[]{:S(2)}) async-start(f16[8,17,8,512]{3,2,1,0:T(8,128)(2,1)} %broadcast_in_dim.66), calls=%async_computation.3 | async-start | bytes 2228224 | tf_op jit(solution)/shard_map/all_to_all | solution.py:40
  96.3 2.6 %select_reduce_fusion = (f32[]{:T(128)}, f32[512,512]{1,0:T(8,128)}) fusion(f32[512,512]{1,0:T(8,128)S(1)} %fusion.31), kind=kOutput, calls=%fused_computation.23 | convolution fusion | flops 806092800 | bytes 2097156 | tf_op jit(solution)/shard_map/dot_general | solution.py:48
  99.6 1.7 %dynamic-slice_bitcast_fusion = f32[1,128,512]{2,1,0:T(8,128)} fusion(f32[512,512]{1,0:T(8,128)} %copy-done.1, s32[]{:T(128)S(6)} %select_n.143), kind=kLoop, calls=%fused_computation.27 | loop fusion | bytes 524292 | tf_op jit(solution)/shard_map/broadcast_in_dim | solution.py:121
  101.3 2.3 %fusion.1 = f32[512,512]{1,0:T(8,128)S(1)} fusion(f32[512,512]{1,0:T(8,128)} %get-tuple-element.24, f32[512,512]{1,0:T(8,128)S(1)} %fusion.31, f32[]{:T(128)S(6)} %mul.171, f32[]{:T(128)S(6)} %div.78), kind=kOutput, calls=%fused_computation.8 | convolution fusion | flops 806879232 | bytes 3145736 | tf_op jit(solution)/shard_map/dot_general | solution.py:117
  103.6 1.0 fusion.32
  104.6 1.0 fusion
  105.6 1.0 fusion.33
  106.7 1.1 fusion.3
  107.8 0.6 fusion.14
  108.4 3.6 %all-to-all-done.3 = f16[8,17,8,512]{3,2,1,0:T(8,128)(2,1)S(1)} async-done(((f16[8,17,8,512]{3,2,1,0:T(8,128)(2,1)}), f16[8,17,8,512]{3,2,1,0:T(8,128)(2,1)S(1)}, u32[]{:S(2)}, u32[]{:S(2)}) %all-to-all-start.3) | async-done | bytes 1114144 | tf_op jit(solution)/shard_map/all_to_all | solution.py:40
  112.0 0.1 copy.25
  112.1 1.0 gather_fusion.1
  113.1 0.1 select_reduce_fusion.2
  113.2 1.5 %convert_multiply_fusion = f32[128,8,512]{2,1,0:T(8,128)} fusion(f16[128,8,512]{2,1,0:T(8,128)(2,1)S(1)} %gather_fusion.1, f32[128]{0:T(128)S(1)} %select_reduce_fusion.2), kind=kLoop, calls=%fused_computation.3 | loop fusion | flops 1048576 | bytes 3146240 | tf_op jit(solution)/shard_map/mul | solution.py:102
  (11 shorter events, 0.2 us)
Async XLA Ops:
  0.6 1.2 %copy-start = (bf16[1,128,8,512]{3,2,1,0:T(8,128)(2,1)S(1)}, bf16[1,128,8,512]{3,2,1,0:T(8,128)(2,1)}, u32[]{:S(2)}) copy-start(bf16[1,128,8,512]{3,2,1,0:T(8,128)(2,1)} %param.7) | copy-start | bytes 3145732
  1.9 7.5 %copy-start.4 = (f32[1,128,512]{2,1,0:T(8,128)S(1)}, f32[1,128,512]{2,1,0:T(8,128)}, u32[]{:S(2)}) copy-start(f32[1,128,512]{2,1,0:T(8,128)} %param.11) | copy-start | bytes 786436
  1.9 7.6 %copy-start.5 = (f32[1,128,512]{2,1,0:T(8,128)S(1)}, f32[1,128,512]{2,1,0:T(8,128)}, u32[]{:S(2)}) copy-start(f32[1,128,512]{2,1,0:T(8,128)} %param.12) | copy-start | bytes 786436
  3.6 27.8 %all-to-all-start = ((bf16[8,16,8,512]{3,2,1,0:T(8,128)(2,1)}), bf16[8,16,8,512]{3,2,1,0:T(8,128)(2,1)}, u32[]{:S(2)}, u32[]{:S(2)}) async-start(bf16[8,16,8,512]{3,2,1,0:T(8,128)(2,1)} %bitcast.3), calls=%async_computation | async-start | bytes 2097152 | tf_op jit(solution)/shard_map/all_to_all | solution.py:40
  9.4 20.0 %copy-start.9 = (s32[128]{0:T(128)S(1)}, s32[128]{0:T(128)}, u32[]{:S(2)}) copy-start(s32[128]{0:T(128)} %param.13) | copy-start | bytes 1540
  9.5 20.0 %copy-start.2 = (f32[2,128,512]{2,1,0:T(8,128)}, f32[2,128,512]{2,1,0:T(8,128)S(1)}, u32[]{:S(2)}) copy-start(f32[2,128,512]{2,1,0:T(8,128)S(1)} %constant_dynamic-update-slice_fusion) | copy-start | bytes 1572868
  9.5 12.4 %collective-permute-start = (f32[2,128,512]{2,1,0:T(8,128)S(1)}, f32[2,128,512]{2,1,0:T(8,128)S(1)}, u32[]{:S(2)}, u32[]{:S(2)}) collective-permute-start(f32[2,128,512]{2,1,0:T(8,128)S(1)} %constant_dynamic-update-slice_fusion), channel_id=1, source_target_pairs={{0,2},{1,3},{2,0},{3,1},{4,6},{5,7},{6,4},{7,5},{8,10},{9,11},{10,... | collective-permute-start | bytes 1572872 | tf_op jit(solution)/shard_map/ppermute | solution.py:44
  21.9 7.6 %copy-start.3 = (f32[2,128,512]{2,1,0:T(8,128)}, f32[2,128,512]{2,1,0:T(8,128)S(1)}, u32[]{:S(2)}) copy-start(f32[2,128,512]{2,1,0:T(8,128)S(1)} %collective-permute-done) | copy-start | bytes 1572868
  23.0 24.6 %collective-permute-start.1 = (f32[2,2,128,512]{3,2,0,1:T(8,128)}, f32[2,2,128,512]{3,2,0,1:T(8,128)}, u32[]{:S(2)}, u32[]{:S(2)}) collective-permute-start(f32[2,2,128,512]{3,2,0,1:T(8,128)} %maximum_select_fusion.1), channel_id=1, source_target_pairs={{0,1},{1,0},{2,3},{3,2},{4,5},{5,4},{6,7},{7,6},{8,9},{9,8},{10,11... | collective-permute-start | bytes 3145736 | tf_op jit(solution)/shard_map/ppermute | solution.py:44
  33.4 26.1 %all-to-all-start.1 = ((f32[16,8,512]{2,1,0:T(8,128)}), f32[16,8,512]{2,1,0:T(8,128)S(1)}, u32[]{:S(2)}, u32[]{:S(2)}) async-start(f32[16,8,512]{2,1,0:T(8,128)} %convert_reduce_fusion), calls=%async_computation.1 | async-start | bytes 524288 | tf_op jit(solution)/shard_map/all_to_all | solution.py:40
  49.5 10.4 %copy-start.6 = (f32[1,8,512]{2,1,0:T(8,128)S(1)}, f32[1,8,512]{2,1,0:T(8,128)}, u32[]{:S(2)}) copy-start(f32[1,8,512]{2,1,0:T(8,128)} %param.9) | copy-start | bytes 49156
  49.5 10.4 %copy-start.7 = (f32[1,8,512]{2,1,0:T(8,128)S(1)}, f32[1,8,512]{2,1,0:T(8,128)}, u32[]{:S(2)}) copy-start(f32[1,8,512]{2,1,0:T(8,128)} %param.10) | copy-start | bytes 49156
  49.5 10.4 %copy-start.8 = (f32[1,8,512]{2,1,0:T(8,128)S(1)}, f32[1,8,512]{2,1,0:T(8,128)}, u32[]{:S(2)}) copy-start(f32[1,8,512]{2,1,0:T(8,128)} %param.8) | copy-start | bytes 49156
  68.8 16.6 %all-to-all-start.2 = ((f32[16,8,512]{2,1,0:T(8,128)}), f32[16,8,512]{2,1,0:T(8,128)S(1)}, u32[]{:S(2)}, u32[]{:S(2)}) async-start(f32[16,8,512]{2,1,0:T(8,128)} %broadcast_in_dim.65), calls=%async_computation.2 | async-start | bytes 524288 | tf_op jit(solution)/shard_map/all_to_all | solution.py:40
  74.2 1.0 copy-start.1
  88.0 24.0 %all-to-all-start.3 = ((f16[8,17,8,512]{3,2,1,0:T(8,128)(2,1)}), f16[8,17,8,512]{3,2,1,0:T(8,128)(2,1)S(1)}, u32[]{:S(2)}, u32[]{:S(2)}) async-start(f16[8,17,8,512]{3,2,1,0:T(8,128)(2,1)} %broadcast_in_dim.66), calls=%async_computation.3 | async-start | bytes 2228224 | tf_op jit(solution)/shard_map/all_to_all | solution.py:40
